TPU v7x, 32 devices: a whole 2x2x4 slice. The times are simulated.
32 devices in a mesh: dp: 8 (over z, x), fsdp: 4 (over y, core).
Axes of the slice: x: 2, y: 2, z: 4, core: 2. Of those that a mesh axis runs over, the one named last changes fastest.
Arguments:
- tokens: bfloat16 [64, 512, 768], P(('dp', 'fsdp')), may hold values from -6 to 6
- segments: int32 [64, 512], P(('dp', 'fsdp')), may hold values from 0 to 11, never falling along the last dimension, each value on 1 to 256 neighbouring positions
- w_query: bfloat16 [768, 768], P(('dp', 'fsdp')), may hold values from -0.21875 to 0.21875
- w_key: bfloat16 [768, 768], P(('dp', 'fsdp')), may hold values from -0.21875 to 0.21875
- w_value: bfloat16 [768, 768], P(('dp', 'fsdp')), may hold values from -0.21875 to 0.21875
- w_output: bfloat16 [768, 768], P(('dp', 'fsdp')), may hold values from -1.25 to 1.25
- w_inner: bfloat16 [768, 3072], P(('dp', 'fsdp')), may hold values from -0.21875 to 0.21875
- w_outer: bfloat16 [3072, 768], P(('dp', 'fsdp')), may hold values from -0.109375 to 0.109375
- down_query: bfloat16 [768, 8], P(('dp', 'fsdp')), may hold values from -0.21875 to 0.21875
- down_value: bfloat16 [768, 8], P(('dp', 'fsdp')), may hold values from -0.21875 to 0.21875
- up_query: bfloat16 [8, 768], replicated, may hold values from -0.59765625 to 0.59765625
- up_value: bfloat16 [8, 768], replicated, may hold values from -0.59765625 to 0.59765625
- norm1_gain: float32 [768], replicated, may hold values from 0.5 to 1.5
- norm1_shift: float32 [768], replicated, may hold values from -1.5 to 1.5
- norm2_gain: float32 [768], replicated, may hold values from 0.5 to 1.5
- norm2_shift: float32 [768], replicated, may hold values from -1.5 to 1.5
- out_grad: bfloat16 [64, 512, 768], P(('dp', 'fsdp')), may hold values from -6 to 6
Outputs:
- layer_out: bfloat16 [64, 512, 768], P(('dp', 'fsdp'))
- tokens_grad: bfloat16 [64, 512, 768], P(('dp', 'fsdp'))
- up_query_grad: float32 [8, 768], replicated
- up_value_grad: float32 [8, 768], replicated
Inputs may be any that keep to these rules, and one draw needn't show every extreme that they name: `segments`: within each packed row the segment numbers never fall; each item spans 1 to 256 positions, and some item spans exactly 256.
All inputs are finite; a program needn't handle non-finite values.
Results may differ from a plain program's by a relative error of at most 0.014.
The roundings to bfloat16 on the way count: a program that leaves them out, or rounds other values in their place, can miss the bound.
Values may be sent and summed in bfloat16 or wider, within the bound.
A program may use at most 128 MiB of HBM per device.

v0:
```python
import jax
import jax.numpy as jnp
from jax import lax
from jax.sharding import PartitionSpec as P

H = 12
HD = 64


def gelu_exact(values):
    return jax.nn.gelu(values, approximate=False)


def normalize(values):
    center = values - jnp.mean(values, axis=-1, keepdims=True)
    scaler = lax.rsqrt(jnp.mean(center * center, axis=-1, keepdims=True) + 1e-05)
    return (center * scaler, scaler)


def norm_back(grad_normed, normed, scaler):
    first = jnp.mean(grad_normed, axis=-1, keepdims=True)
    second = jnp.mean(grad_normed * normed, axis=-1, keepdims=True)
    return scaler * (grad_normed - first - normed * second)


def row_scores(q_row, k_row, seg_row):
    same = seg_row[:, None] == seg_row[None, :]
    scores = jnp.einsum("qhd,khd->hqk", q_row, k_row, preferred_element_type=jnp.float32) * 0.125
    return jnp.where(same[None], scores, -1e30)


def body(
    tokens,
    segments,
    w_query,
    w_key,
    w_value,
    w_output,
    w_inner,
    w_outer,
    down_query,
    down_value,
    up_query,
    up_value,
    norm1_gain,
    norm1_shift,
    norm2_gain,
    norm2_shift,
    out_grad,
):
    row_count, length, width = tokens.shape
    count = row_count * length
    whole = (
        lax.all_gather(w_query, ("dp", "fsdp"), axis=0, tiled=True),
        lax.all_gather(w_key, ("dp", "fsdp"), axis=0, tiled=True),
        lax.all_gather(w_value, ("dp", "fsdp"), axis=0, tiled=True),
        lax.all_gather(w_output, ("dp", "fsdp"), axis=0, tiled=True),
        lax.all_gather(w_inner, ("dp", "fsdp"), axis=0, tiled=True),
        lax.all_gather(w_outer, ("dp", "fsdp"), axis=0, tiled=True),
        lax.all_gather(down_query, ("dp", "fsdp"), axis=0, tiled=True),
        lax.all_gather(down_value, ("dp", "fsdp"), axis=0, tiled=True),
    )
    wq, wk, wv, wo, win, wout, dq_mat, dv_mat = whole
    tok_rows = tokens.reshape(count, width)
    low_q = jnp.dot(tok_rows, dq_mat, preferred_element_type=jnp.float32).astype(jnp.bfloat16)
    low_v = jnp.dot(tok_rows, dv_mat, preferred_element_type=jnp.float32).astype(jnp.bfloat16)
    queries = (
        jnp.dot(tok_rows, wq, preferred_element_type=jnp.float32)
        + 2.0 * jnp.dot(low_q, up_query, preferred_element_type=jnp.float32)
    ).astype(jnp.bfloat16)
    keys_all = jnp.dot(tok_rows, wk, preferred_element_type=jnp.float32).astype(jnp.bfloat16)
    values_all = (
        jnp.dot(tok_rows, wv, preferred_element_type=jnp.float32)
        + 2.0 * jnp.dot(low_v, up_value, preferred_element_type=jnp.float32)
    ).astype(jnp.bfloat16)
    q_heads = queries.reshape(row_count, length, H, HD)
    k_heads = keys_all.reshape(row_count, length, H, HD)
    v_heads = values_all.reshape(row_count, length, H, HD)

    def attend(items):
        q_row, k_row, v_row, seg_row = items
        masked = row_scores(q_row, k_row, seg_row)
        highest = jnp.max(masked, axis=-1, keepdims=True)
        expos = jnp.exp(masked - highest)
        totals = jnp.sum(expos, axis=-1, keepdims=True)
        probs = (expos / totals).astype(jnp.bfloat16)
        context = jnp.einsum("hqk,khd->qhd", probs, v_row, preferred_element_type=jnp.float32)
        return (context.astype(jnp.bfloat16), highest + jnp.log(totals))

    contexts, log_totals = lax.map(attend, (q_heads, k_heads, v_heads, segments))
    context_rows = contexts.reshape(count, width)
    summed1 = tok_rows.astype(jnp.float32) + jnp.dot(
        context_rows, wo, preferred_element_type=jnp.float32
    )
    normed1, scaler1 = normalize(summed1)
    hidden1 = normed1 * norm1_gain + norm1_shift
    hidden_low = hidden1.astype(jnp.bfloat16)
    inner = jnp.dot(hidden_low, win, preferred_element_type=jnp.float32)
    active = gelu_exact(inner).astype(jnp.bfloat16)
    summed2 = hidden1 + jnp.dot(active, wout, preferred_element_type=jnp.float32)
    normed2, scaler2 = normalize(summed2)
    layer_out = (normed2 * norm2_gain + norm2_shift).astype(jnp.bfloat16)
    second = (
        lax.all_gather(w_query, ("dp", "fsdp"), axis=0, tiled=True),
        lax.all_gather(w_key, ("dp", "fsdp"), axis=0, tiled=True),
        lax.all_gather(w_value, ("dp", "fsdp"), axis=0, tiled=True),
        lax.all_gather(w_output, ("dp", "fsdp"), axis=0, tiled=True),
        lax.all_gather(w_inner, ("dp", "fsdp"), axis=0, tiled=True),
        lax.all_gather(w_outer, ("dp", "fsdp"), axis=0, tiled=True),
        lax.all_gather(down_query, ("dp", "fsdp"), axis=0, tiled=True),
        lax.all_gather(down_value, ("dp", "fsdp"), axis=0, tiled=True),
    )
    wq, wk, wv, wo, win, wout, dq_mat, dv_mat = second
    cotangent = out_grad.reshape(count, width).astype(jnp.float32)
    grad_sum2 = norm_back(cotangent * norm2_gain, normed2, scaler2)
    grad_branch = grad_sum2.astype(jnp.bfloat16)
    inner_again = jnp.dot(hidden_low, win, preferred_element_type=jnp.float32)
    gelu_value, gelu_pull = jax.vjp(gelu_exact, inner_again)
    grad_active = jnp.dot(grad_branch, wout.T, preferred_element_type=jnp.float32)
    grad_inner = gelu_pull(grad_active)[0].astype(jnp.bfloat16)
    grad_hidden = grad_sum2 + jnp.dot(grad_inner, win.T, preferred_element_type=jnp.float32)
    grad_sum1 = norm_back(grad_hidden * norm1_gain, normed1, scaler1)
    grad_attended = grad_sum1.astype(jnp.bfloat16)
    grad_context = jnp.dot(grad_attended, wo.T, preferred_element_type=jnp.float32).astype(
        jnp.bfloat16
    )
    grad_heads = grad_context.reshape(row_count, length, H, HD)

    def attend_back(items):
        q_row, k_row, v_row, seg_row, lse_row, grad_row = items
        masked = row_scores(q_row, k_row, seg_row)
        probs = jnp.exp(masked - lse_row)
        grad_v = jnp.einsum(
            "hqk,qhd->khd", probs.astype(jnp.bfloat16), grad_row, preferred_element_type=jnp.float32
        )
        grad_probs = jnp.einsum("qhd,khd->hqk", grad_row, v_row, preferred_element_type=jnp.float32)
        inner_sum = jnp.sum(grad_probs * probs, axis=-1, keepdims=True)
        grad_scores = (probs * (grad_probs - inner_sum)).astype(jnp.bfloat16)
        grad_q = (
            jnp.einsum("hqk,khd->qhd", grad_scores, k_row, preferred_element_type=jnp.float32)
            * 0.125
        )
        grad_k = (
            jnp.einsum("hqk,qhd->khd", grad_scores, q_row, preferred_element_type=jnp.float32)
            * 0.125
        )
        return (
            grad_q.astype(jnp.bfloat16),
            grad_k.astype(jnp.bfloat16),
            grad_v.astype(jnp.bfloat16),
        )

    grad_qh, grad_kh, grad_vh = lax.map(
        attend_back, (q_heads, k_heads, v_heads, segments, log_totals, grad_heads)
    )
    grad_query = grad_qh.reshape(count, width)
    grad_key = grad_kh.reshape(count, width)
    grad_value = grad_vh.reshape(count, width)
    grad_low_q = (2.0 * jnp.dot(grad_query, up_query.T, preferred_element_type=jnp.float32)).astype(
        jnp.bfloat16
    )
    grad_low_v = (2.0 * jnp.dot(grad_value, up_value.T, preferred_element_type=jnp.float32)).astype(
        jnp.bfloat16
    )
    grad_tokens = grad_sum1 + jnp.dot(grad_query, wq.T, preferred_element_type=jnp.float32)
    grad_tokens = grad_tokens + jnp.dot(grad_key, wk.T, preferred_element_type=jnp.float32)
    grad_tokens = grad_tokens + jnp.dot(grad_value, wv.T, preferred_element_type=jnp.float32)
    grad_tokens = grad_tokens + jnp.dot(grad_low_q, dq_mat.T, preferred_element_type=jnp.float32)
    grad_tokens = grad_tokens + jnp.dot(grad_low_v, dv_mat.T, preferred_element_type=jnp.float32)
    local_q = 2.0 * jnp.einsum("tr,td->rd", low_q, grad_query, preferred_element_type=jnp.float32)
    local_v = 2.0 * jnp.einsum("tr,td->rd", low_v, grad_value, preferred_element_type=jnp.float32)
    total_q, total_v = lax.psum((local_q, local_v), ("dp", "fsdp"))
    return (
        layer_out.reshape(row_count, length, width),
        grad_tokens.astype(jnp.bfloat16).reshape(row_count, length, width),
        total_q,
        total_v,
    )


def solution(mesh):
    placed = (
        P(("dp", "fsdp"), None, None),
        P(("dp", "fsdp"), None),
        P(("dp", "fsdp"), None),
        P(("dp", "fsdp"), None),
        P(("dp", "fsdp"), None),
        P(("dp", "fsdp"), None),
        P(("dp", "fsdp"), None),
        P(("dp", "fsdp"), None),
        P(("dp", "fsdp"), None),
        P(("dp", "fsdp"), None),
        P(),
        P(),
        P(),
        P(),
        P(),
        P(),
        P(("dp", "fsdp"), None, None),
    )
    return jax.shard_map(
        body,
        mesh=mesh,
        in_specs=placed,
        out_specs=(P(("dp", "fsdp"), None, None), P(("dp", "fsdp"), None, None), P(), P()),
        check_vma=False,
    )
```

profile of v0, /device:TPU:0, one launch (start us, length us, event | category | flops | bytes accessed | tf_op | source)
XLA Modules:
  0.0 558.4 jit_solution(10017231867190146173)
XLA Ops:
  11.2 43.6 %all-gather = bf16[32,24,8]{1,2,0:T(8,128)(2,1)S(1)} all-gather(bf16[1,24,8]{1,2,0:T(8,128)(2,1)} %bitcast.217), channel_id=1, replica_groups=mesh['dp'=8,'fsdp'=4] {'dp','fsdp'}, dimensions={0}, use_global_device_ids=true | all-gather | bytes 12672 | tf_op jit(solution)/shard_map/all_gather | solution.py:61
  55.0 37.1 %all-gather.1 = bf16[32,24,8]{1,2,0:T(8,128)(2,1)S(1)} all-gather(bf16[1,24,8]{1,2,0:T(8,128)(2,1)} %bitcast.218), channel_id=1, replica_groups=mesh['dp'=8,'fsdp'=4] {'dp','fsdp'}, dimensions={0}, use_global_device_ids=true | all-gather | bytes 12672 | tf_op jit(solution)/shard_map/all_gather | solution.py:60
  97.1 2.7 fusion.91
  103.3 2.4 reshape.185
  105.7 2.9 copy.62
  108.5 15.2 %all-gather.11.cloned.1.call-done = bf16[768,768]{1,0:T(8,128)(2,1)} async-done(((bf16[24,768]{1,0:T(8,128)(2,1)}), bf16[768,768]{1,0:T(8,128)(2,1)}) %all-gather.11.cloned.1.call-update) | async-done | bytes 1179664 | tf_op jit(solution)/shard_map/all_gather | solution.py:54
  123.8 2.7 fusion.92
  129.9 2.4 reshape.186
  134.0 45.7 %all-gather.13.cloned.1.call-done = bf16[768,768]{1,0:T(8,128)(2,1)} async-done(((bf16[24,768]{1,0:T(8,128)(2,1)}), bf16[768,768]{1,0:T(8,128)(2,1)}) %all-gather.13.cloned.1.call-update) | async-done | bytes 1179664 | tf_op jit(solution)/shard_map/all_gather | solution.py:55
  179.7 3.8 convolution_convert_fusion.1
  185.3 2.4 reshape.187
  190.7 20.9 %while.26 = (s32[]{:T(128)}, bf16[2,512,12,64]{1,3,2,0:T(8,128)(2,1)}, f32[2,12,512,1]{2,1,3,0:T(8,128)S(1)}, bf16[2,512,12,64]{1,3,2,0:T(8,128)(2,1)}, s32[2,51...) while((s32[]{:T(128)}, ...), condition=%wide.region_3.4_spmd, body=%wide.region_0.3_spmd.sunk | while | flops 843704320 | bytes 42172508 | solution.py:90
  191.1 2.1 fusion.160
  193.2 2.6 fusion.161
  195.8 5.4 fusion.162
  201.5 2.1 fusion.160
  203.6 2.6 fusion.161
  206.2 5.4 fusion.162
  211.6 3.0 copy.65
  216.2 19.4 %all-gather.15.cloned.1.call-done = bf16[768,768]{1,0:T(8,128)(2,1)} async-done(((bf16[24,768]{1,0:T(8,128)(2,1)}), bf16[768,768]{1,0:T(8,128)(2,1)}) %all-gather.15.cloned.1.call-update) | async-done | bytes 1179664 | tf_op jit(solution)/shard_map/all_gather | solution.py:57
  235.6 5.4 fusion.89
  241.0 2.4 multiply_reduce_fusion.5
  243.4 57.5 %all-gather.17.cloned.1.call-done = bf16[768,3072]{1,0:T(8,128)(2,1)} async-done(((bf16[24,3072]{1,0:T(8,128)(2,1)}), bf16[768,3072]{1,0:T(8,128)(2,1)}) %all-gather.17.cloned.1.call-update) | async-done | bytes 4718608 | tf_op jit(solution)/shard_map/all_gather | solution.py:58
  300.9 36.5 %fusion.57 = (f32[1024,3072]{1,0:T(8,128)}, f32[1024,3072]{1,0:T(8,128)}) fusion(bf16[768,3072]{1,0:T(8,128)(2,1)} %all-gather.17.cloned.1.call-done, f32[1024,768]{1,0:T(8,128)} %get-tuple-element.197, f32[768]{0:T(1024)S(1)} %copy-done.39, f32[768]{0:T(1024)S(1)} %copy-done.40, f32[1024]{0:T(1024)S(1)} %add_rsqrt_fusion.1, ...), kind=kOutput, calls=%fused_computation.65 | convolution fusion | flops 5030805504 | bytes 33044480 | tf_op jit(solution)/shard_map/dot_general | solution.py:98
  337.4 28.7 %all-gather.19.cloned.1.call-done = bf16[3072,768]{1,0:T(8,128)(2,1)} async-done(((bf16[96,768]{1,0:T(8,128)(2,1)}), bf16[3072,768]{1,0:T(8,128)(2,1)}) %all-gather.19.cloned.1.call-update) | async-done | bytes 4718608 | tf_op jit(solution)/shard_map/all_gather | solution.py:59
  366.1 15.6 %fusion.90 = (f32[1024]{0:T(1024)S(1)}, f32[1024,768]{1,0:T(8,128)S(1)}) fusion(bf16[3072,768]{1,0:T(8,128)(2,1)} %all-gather.19.cloned.1.call-done, f32[1024,3072]{1,0:T(8,128)} %get-tuple-element.198, f32[1024,3072]{1,0:T(8,128)} %get-tuple-element.199, f32[768]{0:T(1024)S(1)} %copy-done.39, f32[768]{0:T(1024)S(1)} %copy-done.40, ...), kind=kOutput, calls=%fused_computation.140 | convolution fusion | flops 4845992960 | bytes 36194304 | tf_op jit(solution)/shard_map/dot_general | solution.py:100
  384.0 3.1 subtract_multiply_fusion.1
  387.1 22.7 %fusion.88 = (f32[1024]{0:T(1024)S(1)}, f32[1024]{0:T(1024)S(1)}, f32[1024,768]{1,0:T(8,128)}) fusion(f32[1024]{0:T(1024)S(1)} %add_rsqrt_fusion.1, f32[1024,768]{1,0:T(8,128)} %get-tuple-element.197, f32[1024]{0:T(1024)S(1)} %broadcast_multiply_fusion.4, f32[768]{0:T(1024)S(1)} %copy-done.40, f32[1024,768]{1,0:T(8,128)} %get-tuple-element.194, ...), kind=kOutput, calls=%fused_computation.138 | convolution fusion | flops 9714006016 | bytes 44059648 | tf_op jit(solution)/shard_map/dot_general | solution.py:121
  409.9 6.1 %convolution_convert_fusion = bf16[1024,768]{1,0:T(8,128)(2,1)} fusion(bf16[768,768]{1,0:T(8,128)(2,1)} %all-gather.15.cloned.1.call-done, f32[1024,768]{1,0:T(8,128)} %get-tuple-element.202, f32[1024,768]{1,0:T(8,128)} %get-tuple-element.197, f32[1024]{0:T(1024)S(1)} %get-tuple-element.203, f32[1024]{0:T(1024)S(1)} %get-tuple-element.204, ...), kind=kOutput, calls=%fused_computation.103 | convolution fusion | flops 1214251008 | bytes 9060352 | tf_op jit(solution)/shard_map/dot_general | solution.py:124
  416.0 2.6 copy.66
  418.6 3.8 reshape.190
  422.4 2.9 copy.69
  429.3 48.3 %while.27 = (s32[]{:T(128)}, bf16[2,512,12,64]{1,3,2,0:T(8,128)(2,1)}, bf16[2,512,12,64]{1,3,2,0:T(8,128)(2,1)}, bf16[2,512,12,64]{1,3,2,0:T(8,128)(2,1)}, bf16[...) while((s32[]{:T(128)}, ...), condition=%wide.region_14.15_spmd, body=%wide.region_12.14_spmd.sunk | while | flops 2062673920 | bytes 147524944 | solution.py:153
  431.4 6.7 %multiply_reduce_fusion.7 = (f32[12,512]{1,0:T(8,128)S(1)}, f32[12,512,512]{1,2,0:T(8,128)}) fusion(f32[12,512,512]{1,2,0:T(8,128)S(1)} %fusion.171, f32[12,512]{1,0:T(8,128)S(1)} %dynamic-slice_bitcast_fusion.2, pred[512,512]{0,1:T(8,128)(4,1)S(1)} %broadcast_compare_fusion.5, bf16[2,512,12,64]{1,3,2,0:T(8,128)(2,1)S(1)} %copy-done.1, ...), kind=kOutput, calls=%fused_computation.24.clone.1 | convolution fusion | flops 418375680 | bytes 27059200 | tf_op jit(solution)/shard_map/while/body/eval_jaxpr/qhd,khd->hqk/dot_general | solution.py:136
  438.2 6.8 %multiply_convert_fusion.8 = bf16[12,512,512]{1,2,0:T(8,128)(2,1)S(1)} fusion(f32[12,512,512]{1,2,0:T(8,128)} %get-tuple-element.315, f32[12,512,512]{1,2,0:T(8,128)S(1)} %fusion.171, f32[12,512]{1,0:T(8,128)S(1)} %get-tuple-element.316, f32[12,512]{1,0:T(8,128)S(1)} %dynamic-slice_bitcast_fusion.2, pred[512,512]{0,1:T(8,128)(4,1)S(1)} %broadcast_compare_fusion.5), kind=kLoop, calls=%fused_computation.23.clone.1 | loop fusion | flops 18874368 | bytes 31768576 | tf_op jit(solution)/shard_map/while/body/eval_jaxpr/convert_element_type | solution.py:138
  445.0 2.0 fusion.173
  449.4 4.0 fusion.174
  455.5 6.7 %multiply_reduce_fusion.7 = (f32[12,512]{1,0:T(8,128)S(1)}, f32[12,512,512]{1,2,0:T(8,128)}) fusion(f32[12,512,512]{1,2,0:T(8,128)S(1)} %fusion.171, f32[12,512]{1,0:T(8,128)S(1)} %dynamic-slice_bitcast_fusion.2, pred[512,512]{0,1:T(8,128)(4,1)S(1)} %broadcast_compare_fusion.5, bf16[2,512,12,64]{1,3,2,0:T(8,128)(2,1)S(1)} %copy-done.1, ...), kind=kOutput, calls=%fused_computation.24.clone.1 | convolution fusion | flops 418375680 | bytes 27059200 | tf_op jit(solution)/shard_map/while/body/eval_jaxpr/qhd,khd->hqk/dot_general | solution.py:136
  462.2 6.8 %multiply_convert_fusion.8 = bf16[12,512,512]{1,2,0:T(8,128)(2,1)S(1)} fusion(f32[12,512,512]{1,2,0:T(8,128)} %get-tuple-element.315, f32[12,512,512]{1,2,0:T(8,128)S(1)} %fusion.171, f32[12,512]{1,0:T(8,128)S(1)} %get-tuple-element.316, f32[12,512]{1,0:T(8,128)S(1)} %dynamic-slice_bitcast_fusion.2, pred[512,512]{0,1:T(8,128)(4,1)S(1)} %broadcast_compare_fusion.5), kind=kLoop, calls=%fused_computation.23.clone.1 | loop fusion | flops 18874368 | bytes 31768576 | tf_op jit(solution)/shard_map/while/body/eval_jaxpr/convert_element_type | solution.py:138
  469.1 2.0 fusion.173
  473.5 4.0 fusion.174
  477.6 3.0 copy.71
  481.6 2.6 fusion.79
  490.4 40.9 %all-reduce = (f32[8,768]{1,0:T(8,128)}, f32[8,768]{1,0:T(8,128)}) all-reduce(f32[8,768]{1,0:T(8,128)S(1)} %convolution_multiply_fusion.3, f32[8,768]{1,0:T(8,128)S(1)} %convolution_multiply_fusion.2), channel_id=1, replica_groups=mesh['dp'=8,'fsdp'=4] {'dp','fsdp'}, use_global_device_ids=true, to_apply=%region_15.16 | all-reduce | flops 12288 | bytes 98304 | tf_op jit(solution)/shard_map/psum | solution.py:172
  531.3 4.5 fusion.93
  535.8 3.2 fusion.95
  539.1 3.1 fusion.94
  542.3 8.9 %add_convert_fusion.2 = bf16[1024,768]{1,0:T(8,128)(2,1)} fusion(f32[1024,768]{1,0:T(8,128)} %fusion.79, f32[1024,768]{1,0:T(8,128)} %fusion.95, f32[1024,768]{1,0:T(8,128)} %fusion.94, f32[1024,768]{1,0:T(8,128)} %fusion.93, bf16[768,8]{0,1:T(8,128)(2,1)S(1)} %copy-done.19, bf16[1024,768]{0,1:T(8,128)(2,1)S(1)} %bitcast.196, ...), kind=kOutput, calls=%fused_computation.85 | convolution fusion | flops 34619392 | bytes 22061056 | tf_op jit(solution)/shard_map/dot_general | solution.py:169
  (162 shorter events, 46.8 us)
Async XLA Ops:
  7.2 119.3 %copy-start = (bf16[8,768]{1,0:T(8,128)(2,1)S(1)}, bf16[8,768]{1,0:T(8,128)(2,1)}, u32[]{:S(2)}) copy-start(bf16[8,768]{1,0:T(8,128)(2,1)} %param.31) | copy-start | bytes 36868
  7.2 89.9 %copy-start.6 = (bf16[2,512,768]{2,1,0:T(8,128)(2,1)S(1)}, bf16[2,512,768]{2,1,0:T(8,128)(2,1)}, u32[]{:S(2)}) copy-start(bf16[2,512,768]{2,1,0:T(8,128)(2,1)} %param.21) | copy-start | bytes 4718596
  7.2 88.9 %copy-start.25 = (f32[768]{0:T(1024)S(1)}, f32[768]{0:T(1024)}, u32[]{:S(2)}) copy-start(f32[768]{0:T(1024)} %param.35) | copy-start | bytes 9220
  7.2 88.9 %copy-start.4 = (bf16[2,512,768]{2,1,0:T(8,128)(2,1)S(1)}, bf16[2,512,768]{2,1,0:T(8,128)(2,1)}, u32[]{:S(2)}) copy-start(bf16[2,512,768]{2,1,0:T(8,128)(2,1)} %param.37) | copy-start | bytes 4718596
  7.2 89.9 %all-gather.9.cloned.1.call-start = ((), (), s32[]{:S(2)}) async-start(), calls=%async_computation | async-start | bytes 1216512 | tf_op jit(solution)/shard_map/all_gather | solution.py:56
  8.0 115.8 %all-gather.11.cloned.1.call-start = ((), (), s32[]{:S(2)}) async-start(), calls=%async_computation.1 | async-start | bytes 1216512 | tf_op jit(solution)/shard_map/all_gather | solution.py:54
  8.7 171.0 %all-gather.13.cloned.1.call-start = ((), (), s32[]{:S(2)}) async-start(), calls=%async_computation.2 | async-start | bytes 1216512 | tf_op jit(solution)/shard_map/all_gather | solution.py:55
  9.4 226.1 %all-gather.15.cloned.1.call-start = ((), (), s32[]{:S(2)}) async-start(), calls=%async_computation.3 | async-start | bytes 1216512 | tf_op jit(solution)/shard_map/all_gather | solution.py:57
  10.0 290.9 %all-gather.17.cloned.1.call-start = ((), (), s32[]{:S(2)}) async-start(), calls=%async_computation.4 | async-start | bytes 4866048 | tf_op jit(solution)/shard_map/all_gather | solution.py:58
  10.6 355.5 %all-gather.19.cloned.1.call-start = ((), (), s32[]{:S(2)}) async-start(), calls=%async_computation.5 | async-start | bytes 4866048 | tf_op jit(solution)/shard_map/all_gather | solution.py:59
  55.0 44.8 %copy-start.18 = (bf16[768,8]{0,1:T(8,128)(2,1)}, bf16[768,8]{0,1:T(8,128)(2,1)S(1)}, u32[]{:S(2)}) copy-start(bf16[768,8]{0,1:T(8,128)(2,1)S(1)} %reshape.197) | copy-start | bytes 36868
  92.2 7.6 %copy-start.20 = (bf16[768,8]{0,1:T(8,128)(2,1)}, bf16[768,8]{0,1:T(8,128)(2,1)S(1)}, u32[]{:S(2)}) copy-start(bf16[768,8]{0,1:T(8,128)(2,1)S(1)} %reshape.199) | copy-start | bytes 36868
  94.1 5.7 %copy-start.14 = (bf16[1024,8]{0,1:T(8,128)(2,1)}, bf16[1024,8]{0,1:T(8,128)(2,1)S(1)}, u32[]{:S(2)}) copy-start(bf16[1024,8]{0,1:T(8,128)(2,1)S(1)} %convolution_convert_fusion.3) | copy-start | bytes 49156
  96.1 30.4 %copy-start.16 = (bf16[1024,8]{0,1:T(8,128)(2,1)}, bf16[1024,8]{0,1:T(8,128)(2,1)S(1)}, u32[]{:S(2)}) copy-start(bf16[1024,8]{0,1:T(8,128)(2,1)S(1)} %convolution_convert_fusion.2) | copy-start | bytes 49156
  97.1 2.7 copy-start.23
  187.6 3.1 copy-start.22
  241.0 59.9 %copy-start.39 = (f32[768]{0:T(1024)S(1)}, f32[768]{0:T(1024)}, u32[]{:S(2)}) copy-start(f32[768]{0:T(1024)} %param.34) | copy-start | bytes 9220
  241.0 59.9 %copy-start.40 = (f32[768]{0:T(1024)S(1)}, f32[768]{0:T(1024)}, u32[]{:S(2)}) copy-start(f32[768]{0:T(1024)} %param.33) | copy-start | bytes 9220
  241.0 168.9 %copy-start.27 = (f32[1024]{0:T(1024)}, f32[1024]{0:T(1024)S(1)}, u32[]{:S(2)}) copy-start(f32[1024]{0:T(1024)S(1)} %broadcast_multiply_fusion.4) | copy-start | bytes 12292
  243.4 166.5 %copy-start.29 = (f32[1024]{0:T(1024)}, f32[1024]{0:T(1024)S(1)}, u32[]{:S(2)}) copy-start(f32[1024]{0:T(1024)S(1)} %add_rsqrt_fusion.1) | copy-start | bytes 12292
  381.7 1.4 copy-start.5
  382.3 1.8 copy-start.31
  382.3 1.7 copy-start.36
  409.8 6.1 %copy-start.32 = (f32[1024]{0:T(1024)}, f32[1024]{0:T(1024)S(1)}, u32[]{:S(2)}) copy-start(f32[1024]{0:T(1024)S(1)} %get-tuple-element.203) | copy-start | bytes 12292
  409.8 6.1 %copy-start.34 = (f32[1024]{0:T(1024)}, f32[1024]{0:T(1024)S(1)}, u32[]{:S(2)}) copy-start(f32[1024]{0:T(1024)S(1)} %get-tuple-element.204) | copy-start | bytes 12292
  429.3 2.1 copy-start.1
  429.3 2.1 copy-start.2
  438.2 6.8 %copy-start.9 = (bf16[2,512,12,64]{1,3,2,0:T(8,128)(2,1)S(1)}, bf16[2,512,12,64]{1,3,2,0:T(8,128)(2,1)}, u32[]{:S(2)}) copy-start(bf16[2,512,12,64]{1,3,2,0:T(8,128)(2,1)} %get-tuple-element.354) | copy-start | bytes 4718596 | tf_op jit(solution)/shard_map/while
  445.0 2.0 copy-start.7
  447.0 2.3 copy-start.3
  453.4 2.1 copy-start.1
  453.4 2.1 copy-start.2
  462.2 6.8 %copy-start.9 = (bf16[2,512,12,64]{1,3,2,0:T(8,128)(2,1)S(1)}, bf16[2,512,12,64]{1,3,2,0:T(8,128)(2,1)}, u32[]{:S(2)}) copy-start(bf16[2,512,12,64]{1,3,2,0:T(8,128)(2,1)} %get-tuple-element.354) | copy-start | bytes 4718596 | tf_op jit(solution)/shard_map/while
  469.1 2.0 copy-start.7
  471.1 2.3 copy-start.3
  477.6 3.5 copy-start.17
  481.1 3.1 copy-start.12
  484.2 2.1 copy-start.15
  485.8 1.4 copy-start.11
  531.3 4.5 copy-start.37
  535.8 3.2 copy-start.13
  535.8 3.2 copy-start.38
  539.0 3.2 copy-start.19
  539.0 3.2 copy-start.24
  539.1 3.2 copy-start.28
  539.1 3.2 copy-start.30
  539.1 3.2 copy-start.33
  539.1 3.2 copy-start.35
  (6 other events, 7.0 us)
Sparse Core Ops, SparseCore 0:
  11.0 56.7 all-gather.8
  70.7 53.0 all-gather.10
  126.7 53.0 all-gather.12
  182.5 53.0 all-gather.14
  238.3 62.5 all-gather.16
  303.6 62.4 all-gather.18
where the time goes:
time: 566 us; the launch traced here: 558 us
  matrix products  173 us (31%)
  waiting for transfers between devices  170 us (30%)
  blocking collectives  122 us (22%)
  local copies, waits for them, and re-layouts  51.2 us (9%)
  other arithmetic  27 us (5%)
  between operations  15 us (3%)
    all_gather x1, waiting for transfers between devices, body(): lax.all_gather(w_inner, ('dp', 'fsdp'), axis=0, tiled=True)  57.5 us
    all_gather x1, waiting for transfers between devices, body(): lax.all_gather(w_key, ('dp', 'fsdp'), axis=0, tiled=True)  45.7 us
    all_gather x1, blocking collectives, body(): lax.all_gather(down_value, ('dp', 'fsdp'), axis=0, tiled=True)  43.6 us
    psum x1, blocking collectives, body(): total_q, total_v = lax.psum((local_q, local_v), ('dp', 'fsdp'))  40.9 us
    all_gather x1, blocking collectives, body(): lax.all_gather(down_query, ('dp', 'fsdp'), axis=0, tiled=True)  37.1 us
    dot_general x1, matrix products, body(): inner = jnp.dot(hidden_low, win, preferred_element_type=jnp.float32)  36.5 us
    all_gather x1, waiting for transfers between devices, body(): lax.all_gather(w_outer, ('dp', 'fsdp'), axis=0, tiled=True)  28.7 us
    dot_general x1, matrix products, body(): jnp.dot(grad_inner, win.T, preferred_element_type=jnp.float32)  22.7 us
  transfers between devices with their start and end apart: 6, of which 5 were waited for; matrix products, arithmetic and copies ran while one was open for 19% of the time, Pallas kernels for 0%

commit v1 on v0

--- a/solution.py
+++ b/solution.py
@@ -5,6 +5,18 @@
 
 H = 12
 HD = 64
+
+
+def collect(value, axis, dim):
+    ways, here = (lax.axis_size(axis), lax.axis_index(axis))
+    grown, reach = (value, 1)
+    while reach < ways:
+        theirs = lax.ppermute(grown, axis, [(d, d ^ reach) for d in range(ways)])
+        mine_first = jnp.concatenate([grown, theirs], axis=dim)
+        theirs_first = jnp.concatenate([theirs, grown], axis=dim)
+        grown = jnp.where(here & reach == 0, mine_first, theirs_first)
+        reach = 2 * reach
+    return grown
 
 
 def gelu_exact(values):
@@ -51,7 +63,7 @@
     row_count, length, width = tokens.shape
     count = row_count * length
     whole = (
-        lax.all_gather(w_query, ("dp", "fsdp"), axis=0, tiled=True),
+        collect(w_query, ("dp", "fsdp"), 0),
         lax.all_gather(w_key, ("dp", "fsdp"), axis=0, tiled=True),
         lax.all_gather(w_value, ("dp", "fsdp"), axis=0, tiled=True),
         lax.all_gather(w_output, ("dp", "fsdp"), axis=0, tiled=True),

time: 566 us -> 515 us (0.910)
  waiting for transfers between devices: 170 us -> 99.8 us
  blocking collectives: 122 us -> 131 us
  starting transfers between devices: 0.23 us -> 7.16 us
    all_gather x1, waiting for transfers between devices: 45.7 us -> 0.01 us  [body(): lax.all_gather(w_key, ('dp', 'fsdp'), axis=0, tiled=True)]
    all_gather x1, waiting for transfers between devices: 19.4 us -> 3.08 us  [body(): lax.all_gather(w_output, ('dp', 'fsdp'), axis=0, tiled=True)]
    all_gather x1, waiting for transfers between devices: 15.2 us -> 0.01 us  [body(): lax.all_gather(w_query, ('dp', 'fsdp'), axis=0, tiled=True)]
    ppermute x0 -> x5, waiting for transfers between devices: none -> 7.32 us  [collect(): theirs = lax.ppermute(grown, axis, [(d, d ^ reach) for d in range(ways)])]
    ppermute x0 -> x5, starting transfers between devices: none -> 6.93 us  [collect(): theirs = lax.ppermute(grown, axis, [(d, d ^ reach) for d in range(ways)])]
  transfers between devices with their start and end apart: 6 -> 11, of which waited for: 5 -> 6; matrix products, arithmetic and copies ran while one was open for 19% -> 46% of each run, Pallas kernels for 0% -> 0%
where the time goes in v1:
time: 515 us; the launch traced here: 506 us
  matrix products  170 us (33%)
  blocking collectives  131 us (25%)
  waiting for transfers between devices  99.8 us (19%)
  local copies, waits for them, and re-layouts  53.2 us (10%)
  other arithmetic  29.5 us (6%)
  between operations  15.1 us (3%)
  starting transfers between devices  7.16 us (1%)
    all_gather x1, waiting for transfers between devices, body(): lax.all_gather(w_inner, ('dp', 'fsdp'), axis=0, tiled=True)  57.4 us
    all_gather x1, blocking collectives, body(): lax.all_gather(down_value, ('dp', 'fsdp'), axis=0, tiled=True)  48.8 us
    all_gather x1, blocking collectives, body(): lax.all_gather(down_query, ('dp', 'fsdp'), axis=0, tiled=True)  41.4 us
    psum x1, blocking collectives, body(): total_q, total_v = lax.psum((local_q, local_v), ('dp', 'fsdp'))  40.9 us
    dot_general x1, matrix products, body(): inner = jnp.dot(hidden_low, win, preferred_element_type=jnp.float32)  36.5 us
    all_gather x1, waiting for transfers between devices, body(): lax.all_gather(w_outer, ('dp', 'fsdp'), axis=0, tiled=True)  28.8 us
    dot_general x1, matrix products, body(): jnp.dot(grad_inner, win.T, preferred_element_type=jnp.float32)  22.7 us
    dot_general x1, matrix products, body(): jnp.dot(active, wout, preferred_element_type=jnp.float32)  15.6 us
  transfers between devices with their start and end apart: 11, of which 6 were waited for; matrix products, arithmetic and copies ran while one was open for 46% of the time, Pallas kernels for 0%

profile of v1, /device:TPU:0, one launch (start us, length us, event | category | flops | bytes accessed | tf_op | source)
XLA Modules:
  0.0 506.3 jit_solution(8519195184965840696)
XLA Ops:
  13.1 2.9 collective-permute-start.1
  16.0 2.6 collective-permute-done.1
  20.5 3.6 collective-permute-done.2
  27.6 41.4 %all-gather.1 = bf16[32,24,8]{1,2,0:T(8,128)(2,1)S(1)} all-gather(bf16[1,24,8]{1,2,0:T(8,128)(2,1)} %bitcast.220), channel_id=1, replica_groups=mesh['dp'=8,'fsdp'=4] {'dp','fsdp'}, dimensions={0}, use_global_device_ids=true | all-gather | bytes 12672 | tf_op jit(solution)/shard_map/all_gather | solution.py:72
  70.0 48.8 %all-gather = bf16[32,24,8]{1,2,0:T(8,128)(2,1)S(1)} all-gather(bf16[1,24,8]{1,2,0:T(8,128)(2,1)S(1)} %bitcast.221), channel_id=1, replica_groups=mesh['dp'=8,'fsdp'=4] {'dp','fsdp'}, dimensions={0}, use_global_device_ids=true | all-gather | bytes 12672 | tf_op jit(solution)/shard_map/all_gather | solution.py:73
  120.7 2.6 fusion.66
  125.0 2.4 reshape.186
  129.2 2.7 fusion.99
  133.6 2.6 copy.60
  136.2 3.8 reshape.185
  140.1 2.9 copy.65
  143.0 3.8 convolution_convert_fusion.1
  148.5 2.4 reshape.187
  153.9 20.9 %while.26 = (s32[]{:T(128)}, bf16[2,512,12,64]{1,3,2,0:T(8,128)(2,1)}, f32[2,12,512,1]{2,1,3,0:T(8,128)S(1)}, bf16[2,512,12,64]{1,3,2,0:T(8,128)(2,1)}, s32[2,51...) while((s32[]{:T(128)}, ...), condition=%wide.region_3.4_spmd, body=%wide.region_0.3_spmd.sunk | while | flops 843704320 | bytes 42172508 | solution.py:102
  154.3 2.1 fusion.167
  156.5 2.6 fusion.168
  159.1 5.4 %fusion.169 = bf16[2,512,12,64]{1,3,2,0:T(8,128)(2,1)} fusion(bf16[2,512,12,64]{1,3,2,0:T(8,128)(2,1)} %get-tuple-element.326, s32[]{:T(128)} %get-tuple-element.325, f32[12,512,512]{1,2,0:T(8,128)S(1)} %get-tuple-element.303, f32[12,512]{1,0:T(8,128)S(1)} %fusion.168, f32[12,512]{1,0:T(8,128)S(1)} %get-tuple-element.304, ...), kind=kOutput, calls=%fused_computation.8.clone.1 | convolution fusion | flops 418775040 | bytes 14468096 | tf_op jit(solution)/shard_map/while/body/eval_jaxpr/hqk,khd->qhd/dot_general | solution.py:99
  164.7 2.1 fusion.167
  166.8 2.6 fusion.168
  169.4 5.4 %fusion.169 = bf16[2,512,12,64]{1,3,2,0:T(8,128)(2,1)} fusion(bf16[2,512,12,64]{1,3,2,0:T(8,128)(2,1)} %get-tuple-element.326, s32[]{:T(128)} %get-tuple-element.325, f32[12,512,512]{1,2,0:T(8,128)S(1)} %get-tuple-element.303, f32[12,512]{1,0:T(8,128)S(1)} %fusion.168, f32[12,512]{1,0:T(8,128)S(1)} %get-tuple-element.304, ...), kind=kOutput, calls=%fused_computation.8.clone.1 | convolution fusion | flops 418775040 | bytes 14468096 | tf_op jit(solution)/shard_map/while/body/eval_jaxpr/hqk,khd->qhd/dot_general | solution.py:99
  174.8 3.0 copy.68
  179.4 3.1 all-gather.13.cloned.1.call-done
  182.5 5.4 %fusion.97 = (f32[1024]{0:T(1024)S(1)}, f32[1024,768]{1,0:T(8,128)}) fusion(bf16[1024,768]{0,1:T(8,128)(2,1)} %bitcast.215, bf16[768,768]{1,0:T(8,128)(2,1)} %all-gather.13.cloned.1.call-done, bf16[1024,768]{1,0:T(8,128)(2,1)} %bitcast.203), kind=kOutput, calls=%fused_computation.152 | convolution fusion | flops 1210317824 | bytes 7475200 | tf_op jit(solution)/shard_map/dot_general | solution.py:104
  187.9 2.4 multiply_reduce_fusion.5
  190.3 57.4 %all-gather.15.cloned.1.call-done = bf16[768,3072]{1,0:T(8,128)(2,1)} async-done(((bf16[24,3072]{1,0:T(8,128)(2,1)}), bf16[768,3072]{1,0:T(8,128)(2,1)}) %all-gather.15.cloned.1.call-update) | async-done | bytes 4718608 | tf_op jit(solution)/shard_map/all_gather | solution.py:70
  247.8 36.5 %fusion.57 = (f32[1024,3072]{1,0:T(8,128)}, f32[1024,3072]{1,0:T(8,128)}) fusion(bf16[768,3072]{1,0:T(8,128)(2,1)} %all-gather.15.cloned.1.call-done, f32[1024,768]{1,0:T(8,128)} %get-tuple-element.197, f32[768]{0:T(1024)S(1)} %copy-done.37, f32[768]{0:T(1024)S(1)} %copy-done.38, f32[1024]{0:T(1024)S(1)} %add_rsqrt_fusion.1, ...), kind=kOutput, calls=%fused_computation.65 | convolution fusion | flops 5030805504 | bytes 33044480 | tf_op jit(solution)/shard_map/dot_general | solution.py:110
  284.2 28.8 %all-gather.17.cloned.1.call-done = bf16[3072,768]{1,0:T(8,128)(2,1)} async-done(((bf16[96,768]{1,0:T(8,128)(2,1)}), bf16[3072,768]{1,0:T(8,128)(2,1)}) %all-gather.17.cloned.1.call-update) | async-done | bytes 4718608 | tf_op jit(solution)/shard_map/all_gather | solution.py:71
  313.0 15.6 %fusion.98 = (f32[1024]{0:T(1024)S(1)}, f32[1024,768]{1,0:T(8,128)S(1)}) fusion(bf16[3072,768]{1,0:T(8,128)(2,1)} %all-gather.17.cloned.1.call-done, f32[1024,3072]{1,0:T(8,128)} %get-tuple-element.198, f32[1024,3072]{1,0:T(8,128)} %get-tuple-element.199, f32[768]{0:T(1024)S(1)} %copy-done.37, f32[768]{0:T(1024)S(1)} %copy-done.38, ...), kind=kOutput, calls=%fused_computation.153 | convolution fusion | flops 4845992960 | bytes 36194304 | tf_op jit(solution)/shard_map/dot_general | solution.py:112
  330.9 3.1 subtract_multiply_fusion.1
  334.0 22.7 %fusion.96 = (f32[1024]{0:T(1024)S(1)}, f32[1024]{0:T(1024)S(1)}, f32[1024,768]{1,0:T(8,128)}) fusion(f32[1024]{0:T(1024)S(1)} %add_rsqrt_fusion.1, f32[1024,768]{1,0:T(8,128)} %get-tuple-element.197, f32[1024]{0:T(1024)S(1)} %broadcast_multiply_fusion.4, f32[768]{0:T(1024)S(1)} %copy-done.38, f32[1024,768]{1,0:T(8,128)} %get-tuple-element.194, ...), kind=kOutput, calls=%fused_computation.151 | convolution fusion | flops 9714006016 | bytes 44059648 | tf_op jit(solution)/shard_map/dot_general | solution.py:133
  356.8 6.1 %convolution_convert_fusion = bf16[1024,768]{1,0:T(8,128)(2,1)} fusion(bf16[768,768]{1,0:T(8,128)(2,1)} %all-gather.13.cloned.1.call-done, f32[1024,768]{1,0:T(8,128)} %get-tuple-element.202, f32[1024,768]{1,0:T(8,128)} %get-tuple-element.197, f32[1024]{0:T(1024)S(1)} %get-tuple-element.203, f32[1024]{0:T(1024)S(1)} %get-tuple-element.204, ...), kind=kOutput, calls=%fused_computation.104 | convolution fusion | flops 1214251008 | bytes 9060352 | tf_op jit(solution)/shard_map/dot_general | solution.py:136
  362.9 2.6 copy.69
  365.5 3.8 reshape.190
  369.3 2.9 copy.72
  376.2 48.3 %while.27 = (s32[]{:T(128)}, bf16[2,512,12,64]{1,3,2,0:T(8,128)(2,1)}, bf16[2,512,12,64]{1,3,2,0:T(8,128)(2,1)}, bf16[2,512,12,64]{1,3,2,0:T(8,128)(2,1)}, bf16[...) while((s32[]{:T(128)}, ...), condition=%wide.region_14.15_spmd, body=%wide.region_12.14_spmd.sunk | while | flops 2062673920 | bytes 147524944 | solution.py:165
  378.3 6.7 %multiply_reduce_fusion.7 = (f32[12,512]{1,0:T(8,128)S(1)}, f32[12,512,512]{1,2,0:T(8,128)}) fusion(f32[12,512,512]{1,2,0:T(8,128)S(1)} %fusion.178, f32[12,512]{1,0:T(8,128)S(1)} %dynamic-slice_bitcast_fusion.2, pred[512,512]{0,1:T(8,128)(4,1)S(1)} %broadcast_compare_fusion.5, bf16[2,512,12,64]{1,3,2,0:T(8,128)(2,1)S(1)} %copy-done.1, ...), kind=kOutput, calls=%fused_computation.24.clone.1 | convolution fusion | flops 418375680 | bytes 27059200 | tf_op jit(solution)/shard_map/while/body/eval_jaxpr/qhd,khd->hqk/dot_general | solution.py:148
  385.1 6.8 %multiply_convert_fusion.8 = bf16[12,512,512]{1,2,0:T(8,128)(2,1)S(1)} fusion(f32[12,512,512]{1,2,0:T(8,128)} %get-tuple-element.315, f32[12,512,512]{1,2,0:T(8,128)S(1)} %fusion.178, f32[12,512]{1,0:T(8,128)S(1)} %get-tuple-element.316, f32[12,512]{1,0:T(8,128)S(1)} %dynamic-slice_bitcast_fusion.2, pred[512,512]{0,1:T(8,128)(4,1)S(1)} %broadcast_compare_fusion.5), kind=kLoop, calls=%fused_computation.23.clone.1 | loop fusion | flops 18874368 | bytes 31768576 | tf_op jit(solution)/shard_map/while/body/eval_jaxpr/convert_element_type | solution.py:150
  396.3 4.0 fusion.181
  402.4 6.7 %multiply_reduce_fusion.7 = (f32[12,512]{1,0:T(8,128)S(1)}, f32[12,512,512]{1,2,0:T(8,128)}) fusion(f32[12,512,512]{1,2,0:T(8,128)S(1)} %fusion.178, f32[12,512]{1,0:T(8,128)S(1)} %dynamic-slice_bitcast_fusion.2, pred[512,512]{0,1:T(8,128)(4,1)S(1)} %broadcast_compare_fusion.5, bf16[2,512,12,64]{1,3,2,0:T(8,128)(2,1)S(1)} %copy-done.1, ...), kind=kOutput, calls=%fused_computation.24.clone.1 | convolution fusion | flops 418375680 | bytes 27059200 | tf_op jit(solution)/shard_map/while/body/eval_jaxpr/qhd,khd->hqk/dot_general | solution.py:148
  409.1 6.8 %multiply_convert_fusion.8 = bf16[12,512,512]{1,2,0:T(8,128)(2,1)S(1)} fusion(f32[12,512,512]{1,2,0:T(8,128)} %get-tuple-element.315, f32[12,512,512]{1,2,0:T(8,128)S(1)} %fusion.178, f32[12,512]{1,0:T(8,128)S(1)} %get-tuple-element.316, f32[12,512]{1,0:T(8,128)S(1)} %dynamic-slice_bitcast_fusion.2, pred[512,512]{0,1:T(8,128)(4,1)S(1)} %broadcast_compare_fusion.5), kind=kLoop, calls=%fused_computation.23.clone.1 | loop fusion | flops 18874368 | bytes 31768576 | tf_op jit(solution)/shard_map/while/body/eval_jaxpr/convert_element_type | solution.py:150
  420.3 4.0 fusion.181
  424.5 3.1 copy.76
  434.4 40.9 %all-reduce = (f32[8,768]{1,0:T(8,128)}, f32[8,768]{1,0:T(8,128)}) all-reduce(f32[8,768]{1,0:T(8,128)S(1)} %convolution_multiply_fusion.3, f32[8,768]{1,0:T(8,128)S(1)} %convolution_multiply_fusion.2), channel_id=1, replica_groups=mesh['dp'=8,'fsdp'=4] {'dp','fsdp'}, use_global_device_ids=true, to_apply=%region_15.16 | all-reduce | flops 12288 | bytes 98304 | tf_op jit(solution)/shard_map/psum | solution.py:184
  475.3 2.6 fusion.86
  477.9 4.4 fusion.103
  482.3 4.6 fusion.101
  487.0 3.1 fusion.102
  490.1 8.9 %add_convert_fusion.2 = bf16[1024,768]{1,0:T(8,128)(2,1)} fusion(f32[1024,768]{1,0:T(8,128)} %fusion.86, f32[1024,768]{1,0:T(8,128)} %fusion.103, f32[1024,768]{1,0:T(8,128)} %fusion.102, f32[1024,768]{1,0:T(8,128)} %fusion.101, bf16[768,8]{0,1:T(8,128)(2,1)S(1)} %copy-done.20, bf16[1024,768]{0,1:T(8,128)(2,1)S(1)} %bitcast.199, ...), kind=kOutput, calls=%fused_computation.87 | convolution fusion | flops 34619392 | bytes 22061056 | tf_op jit(solution)/shard_map/dot_general | solution.py:181
  (172 shorter events, 51.8 us)
Async XLA Ops:
  7.2 112.9 %copy-start = (bf16[8,768]{1,0:T(8,128)(2,1)S(1)}, bf16[8,768]{1,0:T(8,128)(2,1)}, u32[]{:S(2)}) copy-start(bf16[8,768]{1,0:T(8,128)(2,1)} %param.31) | copy-start | bytes 36868
  7.2 62.0 %copy-start.5 = (bf16[2,512,768]{2,1,0:T(8,128)(2,1)S(1)}, bf16[2,512,768]{2,1,0:T(8,128)(2,1)}, u32[]{:S(2)}) copy-start(bf16[2,512,768]{2,1,0:T(8,128)(2,1)} %param.21) | copy-start | bytes 4718596
  7.2 62.8 %copy-start.35 = (bf16[24,8]{0,1:T(8,128)(2,1)S(1)}, bf16[24,8]{0,1:T(8,128)(2,1)}, u32[]{:S(2)}) copy-start(bf16[24,8]{0,1:T(8,128)(2,1)} %param.30) | copy-start | bytes 1156
  7.2 122.0 %all-gather.9.cloned.1.call-start = ((), (), s32[]{:S(2)}) async-start(), calls=%async_computation | async-start | bytes 1216512 | tf_op jit(solution)/shard_map/all_gather | solution.py:68
  7.9 135.0 %all-gather.11.cloned.1.call-start = ((), (), s32[]{:S(2)}) async-start(), calls=%async_computation.1 | async-start | bytes 1216512 | tf_op jit(solution)/shard_map/all_gather | solution.py:67
  8.7 173.8 %all-gather.13.cloned.1.call-start = ((), (), s32[]{:S(2)}) async-start(), calls=%async_computation.2 | async-start | bytes 1216512 | tf_op jit(solution)/shard_map/all_gather | solution.py:69
  9.4 238.3 %all-gather.15.cloned.1.call-start = ((), (), s32[]{:S(2)}) async-start(), calls=%async_computation.3 | async-start | bytes 4866048 | tf_op jit(solution)/shard_map/all_gather | solution.py:70
  10.0 303.0 %all-gather.17.cloned.1.call-start = ((), (), s32[]{:S(2)}) async-start(), calls=%async_computation.4 | async-start | bytes 4866048 | tf_op jit(solution)/shard_map/all_gather | solution.py:71
  10.6 471.7 %all-gather.19.cloned.1.call-start = ((), (), s32[]{:S(2)}) async-start(), calls=%async_computation.5 | async-start | bytes 1216512 | tf_op jit(solution)/shard_map/all_gather | solution.py:116
  10.6 1.6 collective-permute-start
  13.1 5.5 %collective-permute-start.1 = (bf16[48,768]{1,0:T(8,128)(2,1)S(1)}, bf16[48,768]{1,0:T(8,128)(2,1)S(1)}, u32[]{:S(2)}, u32[]{:S(2)}) collective-permute-start(bf16[48,768]{1,0:T(8,128)(2,1)S(1)} %maximum_select_fusion.5), channel_id=1, source_target_pairs={{0,2},{1,3},{2,0},{3,1},{4,6},{5,7},{6,4},{7,5},{8,10},{9,11},{10,... | collective-permute-start | bytes 221192 | tf_op jit(solution)/shard_map/ppermute | solution.py:14
  18.6 5.5 %collective-permute-start.2 = (bf16[96,768]{1,0:T(8,128)(2,1)S(1)}, bf16[96,768]{1,0:T(8,128)(2,1)S(1)}, u32[]{:S(2)}, u32[]{:S(2)}) collective-permute-start(bf16[96,768]{1,0:T(8,128)(2,1)S(1)} %maximum_select_fusion.4), channel_id=1, source_target_pairs={{0,4},{1,5},{2,6},{3,7},{4,0},{5,1},{6,2},{7,3},{8,12},{9,13},{10,... | collective-permute-start | bytes 442376 | tf_op jit(solution)/shard_map/ppermute | solution.py:14
  24.2 45.5 %collective-permute-start.3 = (bf16[192,768]{1,0:T(8,128)(2,1)S(1)}, bf16[192,768]{1,0:T(8,128)(2,1)S(1)}, u32[]{:S(2)}, u32[]{:S(2)}) collective-permute-start(bf16[192,768]{1,0:T(8,128)(2,1)S(1)} %maximum_select_fusion.3), channel_id=1, source_target_pairs={{0,8},{1,9},{2,10},{3,11},{4,12},{5,13},{6,14},{7,15},{8,0},{9,1},... | collective-permute-start | bytes 884744 | tf_op jit(solution)/shard_map/ppermute | solution.py:14
  69.7 53.6 %copy-start.13 = (bf16[1024,8]{0,1:T(8,128)(2,1)}, bf16[1024,8]{0,1:T(8,128)(2,1)S(1)}, u32[]{:S(2)}) copy-start(bf16[1024,8]{0,1:T(8,128)(2,1)S(1)} %convolution_convert_fusion.2) | copy-start | bytes 49156
  69.9 50.8 %collective-permute-start.4 = (bf16[384,768]{1,0:T(8,128)(2,1)S(1)}, bf16[384,768]{1,0:T(8,128)(2,1)S(1)}, u32[]{:S(2)}, u32[]{:S(2)}) collective-permute-start(bf16[384,768]{1,0:T(8,128)(2,1)S(1)} %maximum_select_fusion.2), channel_id=1, source_target_pairs={{0,16},{1,17},{2,18},{3,19},{4,20},{5,21},{6,22},{7,23},{8,24},{9,... | collective-permute-start | bytes 1769480 | tf_op jit(solution)/shard_map/ppermute | solution.py:14
  118.9 4.4 copy-start.19
  120.0 11.8 %copy-start.15 = (bf16[1024,8]{0,1:T(8,128)(2,1)}, bf16[1024,8]{0,1:T(8,128)(2,1)S(1)}, u32[]{:S(2)}) copy-start(bf16[1024,8]{0,1:T(8,128)(2,1)S(1)} %convolution_convert_fusion.3) | copy-start | bytes 49156
  129.1 2.7 copy-start.22
  150.8 3.1 copy-start.21
  187.9 59.9 %copy-start.37 = (f32[768]{0:T(1024)S(1)}, f32[768]{0:T(1024)}, u32[]{:S(2)}) copy-start(f32[768]{0:T(1024)} %param.34) | copy-start | bytes 9220
  187.9 59.9 %copy-start.38 = (f32[768]{0:T(1024)S(1)}, f32[768]{0:T(1024)}, u32[]{:S(2)}) copy-start(f32[768]{0:T(1024)} %param.33) | copy-start | bytes 9220
  187.9 168.9 %copy-start.25 = (f32[1024]{0:T(1024)}, f32[1024]{0:T(1024)S(1)}, u32[]{:S(2)}) copy-start(f32[1024]{0:T(1024)S(1)} %broadcast_multiply_fusion.4) | copy-start | bytes 12292
  190.3 166.5 %copy-start.27 = (f32[1024]{0:T(1024)}, f32[1024]{0:T(1024)S(1)}, u32[]{:S(2)}) copy-start(f32[1024]{0:T(1024)S(1)} %add_rsqrt_fusion.1) | copy-start | bytes 12292
  356.7 6.1 %copy-start.30 = (f32[1024]{0:T(1024)}, f32[1024]{0:T(1024)S(1)}, u32[]{:S(2)}) copy-start(f32[1024]{0:T(1024)S(1)} %get-tuple-element.203) | copy-start | bytes 12292
  356.7 6.1 %copy-start.32 = (f32[1024]{0:T(1024)}, f32[1024]{0:T(1024)S(1)}, u32[]{:S(2)}) copy-start(f32[1024]{0:T(1024)S(1)} %get-tuple-element.204) | copy-start | bytes 12292
  376.2 2.1 copy-start.1
  376.2 2.1 copy-start.2
  385.1 6.8 %copy-start.9 = (bf16[2,512,12,64]{1,3,2,0:T(8,128)(2,1)S(1)}, bf16[2,512,12,64]{1,3,2,0:T(8,128)(2,1)}, u32[]{:S(2)}) copy-start(bf16[2,512,12,64]{1,3,2,0:T(8,128)(2,1)} %get-tuple-element.354) | copy-start | bytes 4718596 | tf_op jit(solution)/shard_map/while
  391.9 2.0 copy-start.6
  393.9 2.3 copy-start.3
  400.3 2.1 copy-start.1
  400.3 2.1 copy-start.2
  409.1 6.8 %copy-start.9 = (bf16[2,512,12,64]{1,3,2,0:T(8,128)(2,1)S(1)}, bf16[2,512,12,64]{1,3,2,0:T(8,128)(2,1)}, u32[]{:S(2)}) copy-start(bf16[2,512,12,64]{1,3,2,0:T(8,128)(2,1)} %get-tuple-element.354) | copy-start | bytes 4718596 | tf_op jit(solution)/shard_map/while
  416.0 2.0 copy-start.6
  418.0 2.3 copy-start.3
  424.5 3.6 copy-start.8
  428.1 2.1 copy-start.11
  430.1 3.2 copy-start.16
  431.8 2.1 copy-start.14
  431.8 43.5 %copy-start.18 = (bf16[768,8]{0,1:T(8,128)(2,1)S(1)}, bf16[768,8]{0,1:T(8,128)(2,1)}, u32[]{:S(2)}) copy-start(bf16[768,8]{0,1:T(8,128)(2,1)} %copy-done.17) | copy-start | bytes 36868
  482.3 4.6 copy-start.12
  482.3 4.6 copy-start.36
  486.9 3.2 copy-start.20
  486.9 3.2 copy-start.23
  486.9 3.2 copy-start.26
  486.9 3.2 copy-start.28
  486.9 3.2 copy-start.31
  487.0 3.2 copy-start.33
  (9 other events, 11.8 us)
Sparse Core Ops, SparseCore 0:
  10.9 56.8 all-gather.8
  70.8 55.6 all-gather.10
  129.4 53.0 all-gather.12
  185.3 62.4 all-gather.14
  250.5 62.4 all-gather.16
  315.7 52.8 all-gather.18
